TPU v7x, 32 devices: a whole 2x2x4 slice. The times are simulated.
32 devices in a mesh: img: 8 (over y, x, core), seq: 4 (over z).
Axes of the slice: x: 2, y: 2, z: 4, core: 2. Of those that a mesh axis runs over, the one named last changes fastest.
Arguments:
- x_big: bfloat16 [128, 200, 768], P(('img', 'seq')), may hold values from -6 to 6
- x_small: bfloat16 [512, 40, 768], P(('img', 'seq')), may hold values from -6 to 6
- mask_big: int32 [128, 200], P('img'), may hold values from 0 to 1, as said below
- mask_small: int32 [512, 40], P('img'), may hold values from 0 to 1, as said below
- ln1_gain: float32 [768], P('seq'), may hold values from 0.5 to 1.5
- ln1_bias: float32 [768], P('seq'), may hold values from -1.75 to 1.75
- w_qkv: float32 [768, 2304], P('img', 'seq'), may hold values from -0.21875 to 0.21875
- b_qv: float32 [1536], P('seq'), may hold values from -3 to 3
- w_out: float32 [768, 768], P('img', 'seq'), may hold values from -0.625 to 0.625
- b_out: float32 [768], P('seq'), may hold values from -1.75 to 1.75
- ln2_gain: float32 [768], P('seq'), may hold values from 0.5 to 1.5
- ln2_bias: float32 [768], P('seq'), may hold values from -1.75 to 1.75
- w_up: float32 [768, 3072], P('img', 'seq'), may hold values from -0.21875 to 0.21875
- b_up: float32 [3072], P('seq'), may hold values from -3 to 3
- w_down: float32 [3072, 768], P('img', 'seq'), may hold values from -0.109375 to 0.109375
- b_down: float32 [768], P('seq'), may hold values from -1.75 to 1.75
- dy_big: bfloat16 [128, 200, 768], P(('img', 'seq')), may hold values from -6 to 6
- dy_small: bfloat16 [512, 40, 768], P(('img', 'seq')), may hold values from -6 to 6
Outputs:
- y_big: bfloat16 [128, 200, 768], P(('img', 'seq'))
- y_small: bfloat16 [512, 40, 768], P(('img', 'seq'))
- dx_big: bfloat16 [128, 200, 768], P(('img', 'seq'))
- dx_small: bfloat16 [512, 40, 768], P(('img', 'seq'))
- g_ln1_gain: float32 [768], P('seq')
- g_ln1_bias: float32 [768], P('seq')
- g_w_qkv: float32 [768, 2304], P('img', 'seq')
- g_b_qv: float32 [1536], P('seq')
- g_w_out: float32 [768, 768], P('img', 'seq')
- g_b_out: float32 [768], P('seq')
- g_ln2_gain: float32 [768], P('seq')
- g_ln2_bias: float32 [768], P('seq')
- g_w_up: float32 [768, 3072], P('img', 'seq')
- g_b_up: float32 [3072], P('seq')
- g_w_down: float32 [3072, 768], P('img', 'seq')
- g_b_down: float32 [768], P('seq')
Inputs may be any that keep to these rules, and one draw needn't show every extreme that they name: `mask_big`: each 224px crop's mask is 1 on its first 175 to 200 slots and 0 after; some crop has all slots valid and some the fewest. `mask_small`: each 96px crop's mask is 1 on its first 35 to 40 slots and 0 after; some crop has all slots valid and some the fewest.
All inputs are finite; a program needn't handle non-finite values.
Results may differ from a plain program's by a relative error of at most 0.014.
Values may be sent and summed in bfloat16 or wider, within the bound.
A program may use at most 192 MiB of HBM per device.

v0:
```python
import jax
import jax.numpy as jnp
from jax import lax
from jax.sharding import PartitionSpec as P

HEADS = 12
HEAD_DIM = 64
AXES = ("img", "seq")
EPSILON = 1e-06
NEGATIVE = -1e30


def layer_norm(values, gain_vec, shift_vec):
    row_mean = jnp.mean(values, axis=-1, keepdims=True)
    centred = values - row_mean
    variance = jnp.mean(centred * centred, axis=-1, keepdims=True)
    return centred * lax.rsqrt(variance + EPSILON) * gain_vec + shift_vec


def gelu_exact(values):
    return jax.nn.gelu(values, approximate=False)


def head_scores(heads_in, key_valid):
    crop_count, length = (heads_in.shape[0], heads_in.shape[1])
    pieces = heads_in.reshape(crop_count, length, 3, HEADS, HEAD_DIM)
    queries, key_rows, value_rows = (pieces[:, :, 0], pieces[:, :, 1], pieces[:, :, 2])
    raw_scores = jnp.einsum(
        "cqhd,ckhd->chqk", queries, key_rows, preferred_element_type=jnp.float32
    )
    scores = jnp.where(key_valid[:, None, None, :] > 0, raw_scores * HEAD_DIM ** (-0.5), NEGATIVE)
    return (queries, key_rows, value_rows, scores)


def attend(heads_in, key_valid):
    crop_count, length = (heads_in.shape[0], heads_in.shape[1])
    queries, key_rows, value_rows, scores = head_scores(heads_in, key_valid)
    row_max = jnp.max(scores, axis=-1, keepdims=True)
    exponent = jnp.exp(scores - row_max)
    row_total = jnp.sum(exponent, axis=-1, keepdims=True)
    softmax_w = (exponent / row_total).astype(jnp.bfloat16)
    mixed_out = jnp.einsum(
        "chqk,ckhd->cqhd", softmax_w, value_rows, preferred_element_type=jnp.float32
    )
    log_total = row_max + jnp.log(row_total)
    return (mixed_out.astype(jnp.bfloat16).reshape(crop_count * length, -1), log_total)


def attend_back(heads_in, key_valid, log_total, grad_heads):
    crop_count, length = (heads_in.shape[0], heads_in.shape[1])
    queries, key_rows, value_rows, scores = head_scores(heads_in, key_valid)
    softmax_f = jnp.exp(scores - log_total)
    grad_mixed = grad_heads.reshape(crop_count, length, HEADS, HEAD_DIM)
    grad_soft = jnp.einsum(
        "cqhd,ckhd->chqk", grad_mixed, value_rows, preferred_element_type=jnp.float32
    )
    inner_sum = jnp.sum(softmax_f * grad_soft, axis=-1, keepdims=True)
    grad_raw = (softmax_f * (grad_soft - inner_sum) * HEAD_DIM ** (-0.5)).astype(jnp.bfloat16)
    grad_query = jnp.einsum(
        "chqk,ckhd->cqhd", grad_raw, key_rows, preferred_element_type=jnp.float32
    )
    grad_key = jnp.einsum("chqk,cqhd->ckhd", grad_raw, queries, preferred_element_type=jnp.float32)
    grad_value = jnp.einsum(
        "chqk,cqhd->ckhd",
        softmax_f.astype(jnp.bfloat16),
        grad_mixed,
        preferred_element_type=jnp.float32,
    )
    stacked = jnp.stack([grad_query, grad_key, grad_value], axis=2).astype(jnp.bfloat16)
    return stacked.reshape(crop_count * length, -1)


def gather_mats(mats):
    n_img, n_seq = (lax.axis_size("img"), lax.axis_size("seq"))
    flat = jnp.concatenate([m.astype(jnp.bfloat16).reshape(-1, 64) for m in mats], axis=0)
    whole = lax.all_gather(flat, AXES, axis=0, tiled=False)
    outs, at = ([], 0)
    for m in mats:
        rows = m.size // 64
        piece = whole[:, at : at + rows].reshape((n_img, n_seq) + m.shape)
        at += rows
        if m.ndim == 2:
            piece = piece.transpose(0, 2, 1, 3).reshape(n_img * m.shape[0], n_seq * m.shape[1])
        else:
            piece = piece[0].reshape(-1)
        outs.append(piece)
    return outs


def scatter_mats(mats):
    n_img, n_seq = (lax.axis_size("img"), lax.axis_size("seq"))
    blocks = []
    for m in mats:
        rows, cols = (m.shape[0] // n_img, m.shape[1] // n_seq)
        b = m.astype(jnp.bfloat16).reshape(n_img, rows, n_seq, cols).transpose(0, 2, 1, 3)
        blocks.append(b.reshape(n_img * n_seq, -1, 128))
    flat = jnp.concatenate(blocks, axis=1)
    mine = lax.psum_scatter(flat, AXES, scatter_dimension=0, tiled=False)
    outs, at = ([], 0)
    for m, b in zip(mats, blocks):
        piece = mine[at : at + b.shape[1]]
        at += b.shape[1]
        outs.append(piece.reshape(m.shape[0] // n_img, m.shape[1] // n_seq).astype(jnp.float32))
    return outs


def body(
    x_big,
    x_small,
    mask_big,
    mask_small,
    ln1_gain,
    ln1_bias,
    w_qkv,
    b_qv,
    w_out,
    b_out,
    ln2_gain,
    ln2_bias,
    w_up,
    b_up,
    w_down,
    b_down,
    dy_big,
    dy_small,
):
    n_seq = lax.axis_size("seq")
    where = lax.axis_index("seq")
    model_width = x_big.shape[2]
    big_crops, big_length = (x_big.shape[0], x_big.shape[1])
    small_crops, small_length = (x_small.shape[0], x_small.shape[1])
    big_rows = big_crops * big_length
    mask_big = lax.dynamic_slice_in_dim(mask_big, where * big_crops, big_crops, 0)
    mask_small = lax.dynamic_slice_in_dim(mask_small, where * small_crops, small_crops, 0)
    qkv_full, gain_one, shift_one, bias_qv, bias_out, gain_two, shift_two, bias_up, bias_down = (
        gather_mats([w_qkv, ln1_gain, ln1_bias, b_qv, b_out, ln2_gain, ln2_bias, b_up, b_down])
    )
    out_full, up_full, down_full = gather_mats([w_out, w_up, w_down])
    gain_one, shift_one, bias_qv, bias_out, gain_two, shift_two, bias_up, bias_down = tuple(
        (
            vec.astype(jnp.float32)
            for vec in (
                gain_one,
                shift_one,
                bias_qv,
                bias_out,
                gain_two,
                shift_two,
                bias_up,
                bias_down,
            )
        )
    )
    tokens = jnp.concatenate(
        [x_big.reshape(big_rows, model_width), x_small.reshape(-1, model_width)], axis=0
    ).astype(jnp.float32)
    normed_one, pull_one = jax.vjp(layer_norm, tokens, gain_one, shift_one)
    input_one = normed_one.astype(jnp.bfloat16)
    bias_qkv = jnp.concatenate(
        [bias_qv[:model_width], jnp.zeros((model_width,), jnp.float32), bias_qv[model_width:]]
    )
    projected = (
        jnp.dot(input_one, qkv_full, preferred_element_type=jnp.float32) + bias_qkv
    ).astype(jnp.bfloat16)
    heads_big = projected[:big_rows].reshape(big_crops, big_length, -1)
    heads_small = projected[big_rows:].reshape(small_crops, small_length, -1)
    mixed_big, total_big = attend(heads_big, mask_big)
    mixed_small, total_small = attend(heads_small, mask_small)
    mixed_tok = jnp.concatenate([mixed_big, mixed_small], axis=0)
    middle = tokens + jnp.dot(mixed_tok, out_full, preferred_element_type=jnp.float32) + bias_out
    normed_two, pull_two = jax.vjp(layer_norm, middle, gain_two, shift_two)
    input_two = normed_two.astype(jnp.bfloat16)
    up_proj = jnp.dot(input_two, up_full, preferred_element_type=jnp.float32) + bias_up
    activated_f, pull_act = jax.vjp(gelu_exact, up_proj)
    activated = activated_f.astype(jnp.bfloat16)
    result = middle + jnp.dot(activated, down_full, preferred_element_type=jnp.float32) + bias_down
    grad_out = jnp.concatenate(
        [dy_big.reshape(big_rows, model_width), dy_small.reshape(-1, model_width)], axis=0
    )
    grad_down = jnp.einsum("ti,tj->ij", activated, grad_out, preferred_element_type=jnp.float32)
    grad_bias_down = jnp.sum(grad_out.astype(jnp.float32), axis=0)
    grad_act = jnp.einsum("tj,ij->ti", grad_out, down_full, preferred_element_type=jnp.float32)
    (grad_up_f,) = pull_act(grad_act)
    grad_up_b = grad_up_f.astype(jnp.bfloat16)
    grad_upw = jnp.einsum("ti,tj->ij", input_two, grad_up_b, preferred_element_type=jnp.float32)
    grad_bias_up = jnp.sum(grad_up_b.astype(jnp.float32), axis=0)
    grad_in_two = jnp.einsum("tj,ij->ti", grad_up_b, up_full, preferred_element_type=jnp.float32)
    grad_middle_ln, grad_gain_two, grad_shift_two = pull_two(grad_in_two)
    grad_middle = grad_out.astype(jnp.float32) + grad_middle_ln
    grad_branch = grad_middle.astype(jnp.bfloat16)
    grad_bias_out = jnp.sum(grad_branch.astype(jnp.float32), axis=0)
    grad_outw = jnp.einsum("ti,tj->ij", mixed_tok, grad_branch, preferred_element_type=jnp.float32)
    grad_mixed = jnp.einsum(
        "tj,ij->ti", grad_branch, out_full, preferred_element_type=jnp.float32
    ).astype(jnp.bfloat16)
    grad_projected = jnp.concatenate(
        [
            attend_back(heads_big, mask_big, total_big, grad_mixed[:big_rows]),
            attend_back(heads_small, mask_small, total_small, grad_mixed[big_rows:]),
        ],
        axis=0,
    )
    grad_qkvw = jnp.einsum(
        "ti,tj->ij", input_one, grad_projected, preferred_element_type=jnp.float32
    )
    grad_proj_sums = jnp.sum(grad_projected.astype(jnp.float32), axis=0)
    grad_bias_qv = jnp.concatenate(
        [grad_proj_sums[:model_width], grad_proj_sums[2 * model_width :]]
    )
    grad_in_one = jnp.einsum(
        "tj,ij->ti", grad_projected, qkv_full, preferred_element_type=jnp.float32
    )
    grad_tokens_ln, grad_gain_one, grad_shift_one = pull_one(grad_in_one)
    grad_tokens = (grad_middle + grad_tokens_ln).astype(jnp.bfloat16)
    vectors = (
        grad_gain_one,
        grad_shift_one,
        grad_bias_qv,
        grad_bias_out,
        grad_gain_two,
        grad_shift_two,
        grad_bias_up,
        grad_bias_down,
    )
    vector_sums = lax.psum(jnp.concatenate(vectors), AXES)
    vec_out, at = ([], 0)
    for v in vectors:
        width = v.shape[0] // n_seq
        vec_out.append(lax.dynamic_slice(vector_sums, (at + where * width,), (width,)))
        at += v.shape[0]
    g_up, g_down = scatter_mats([grad_upw, grad_down])
    g_qkv, g_out = scatter_mats([grad_qkvw, grad_outw])
    y_big = result[:big_rows].reshape(big_crops, big_length, model_width).astype(jnp.bfloat16)
    y_small = result[big_rows:].reshape(small_crops, small_length, model_width).astype(jnp.bfloat16)
    dx_big = grad_tokens[:big_rows].reshape(big_crops, big_length, model_width)
    dx_small = grad_tokens[big_rows:].reshape(small_crops, small_length, model_width)
    return (
        y_big,
        y_small,
        dx_big,
        dx_small,
        vec_out[0],
        vec_out[1],
        g_qkv,
        vec_out[2],
        g_out,
        vec_out[3],
        vec_out[4],
        vec_out[5],
        g_up,
        vec_out[6],
        g_down,
        vec_out[7],
    )


def solution(mesh):
    rows3 = P(AXES, None, None)
    placed = (
        rows3,
        rows3,
        P("img", None),
        P("img", None),
        P("seq"),
        P("seq"),
        P("img", "seq"),
        P("seq"),
        P("img", "seq"),
        P("seq"),
        P("seq"),
        P("seq"),
        P("img", "seq"),
        P("seq"),
        P("img", "seq"),
        P("seq"),
        rows3,
        rows3,
    )
    return jax.shard_map(
        body,
        mesh=mesh,
        in_specs=placed,
        out_specs=(rows3,) * 4
        + (
            P("seq"),
            P("seq"),
            P("img", "seq"),
            P("seq"),
            P("img", "seq"),
            P("seq"),
            P("seq"),
            P("seq"),
            P("img", "seq"),
            P("seq"),
            P("img", "seq"),
            P("seq"),
        ),
        check_vma=False,
    )
```

profile of v0, /device:TPU:0, one launch (start us, length us, event | category | flops | bytes accessed | tf_op | source)
XLA Modules:
  0.0 870.6 jit_solution(1051177203787296150)
XLA Ops:
  25.0 55.9 %all-gather.7.cloned.1.call-done = bf16[32,900,64]{1,2,0:T(8,128)(2,1)} async-done(((bf16[1,900,64]{1,2,0:T(8,128)(2,1)}), bf16[32,900,64]{1,2,0:T(8,128)(2,1)}) %all-gather.7.cloned.1.call-update) | async-done | bytes 3686416 | tf_op jit(solution)/shard_map/all_gather | solution.py:76
  97.2 10.8 %reshape.350 = bf16[8,4,96,576]{3,2,1,0:T(8,128)(2,1)} reshape(bf16[32,864,64]{2,1,0:T(8,128)(2,1)} %copy.143) | data formatting | bytes 7077888 | tf_op jit(solution)/shard_map/reshape | solution.py:80
  122.0 9.1 %fusion.8 = bf16[1440,2304]{1,0:T(8,128)(2,1)S(1)} fusion(bf16[768,2304]{1,0:T(8,128)(2,1)} %reshape.351, f32[2304]{0:T(1024)S(1)} %pad_maximum_fusion.12, f32[768]{0:T(1024)S(1)} %reshape.378, f32[768]{0:T(1024)S(1)} %reshape.377, f32[1440]{0:T(1024)S(1)} %fusion.103, f32[1440]{0:T(1024)S(1)} %broadcast_multiply_fusion.1, ...), kind=kOutput, calls=%fused_computation.22 | convolution fusion | flops 5112668160 | bytes 12413184 | tf_op jit(solution)/shard_map/dot_general | solution.py:163
  136.7 9.8 %reshape_reshape.9 = bf16[16,40,3,12,64]{4,3,2,1,0:T(8,128)(2,1)} reshape(bf16[640,2304]{1,0:T(8,128)(2,1)} %slice.190) | data formatting | bytes 5898240 | tf_op jit(solution)/shard_map/reshape;reshape | solution.py:26
  168.5 12.1 %reshape.398 = bf16[4,200,3,12,64]{4,3,2,1,0:T(8,128)(2,1)} reshape(bf16[800,2304]{1,0:T(8,128)(2,1)} %slice.186) | data formatting | bytes 7372800 | tf_op jit(solution)/shard_map/reshape;reshape | solution.py:26
  239.9 14.1 %fusion.135 = (bf16[32,1152,64]{1,2,0:T(8,128)(2,1)}, bf16[32,1152,64]{1,2,0:T(8,128)(2,1)}) fusion(bf16[32,2592,64]{1,2,0:T(8,128)(2,1)} %all-gather.9.cloned.1.call-done), kind=kLoop, calls=%fused_computation.187 | loop fusion | bytes 18874368 | tf_op jit(solution)/shard_map/slice | solution.py:80
  254.0 9.6 %copy.174 = bf16[32,1152,64]{2,1,0:T(8,128)(2,1)} copy(bf16[32,1152,64]{1,2,0:T(8,128)(2,1)} %get-tuple-element.77) | data formatting | bytes 9437184 | tf_op jit(solution)/shard_map/slice | solution.py:80
  263.7 15.5 %reshape.361 = bf16[8,4,384,192]{3,2,1,0:T(8,128)(2,1)} reshape(bf16[32,1152,64]{2,1,0:T(8,128)(2,1)} %copy.174) | data formatting | bytes 9437184 | tf_op jit(solution)/shard_map/reshape | solution.py:80
  293.6 9.6 %copy.170 = bf16[32,1152,64]{2,1,0:T(8,128)(2,1)} copy(bf16[32,1152,64]{1,2,0:T(8,128)(2,1)} %get-tuple-element.78) | data formatting | bytes 9437184 | tf_op jit(solution)/shard_map/slice | solution.py:80
  303.3 13.4 %reshape.359 = bf16[8,4,96,768]{3,2,1,0:T(8,128)(2,1)} reshape(bf16[32,1152,64]{2,1,0:T(8,128)(2,1)} %copy.170) | data formatting | bytes 9437184 | tf_op jit(solution)/shard_map/reshape | solution.py:80
  328.1 48.1 %multiply_convert_fusion = (bf16[1440,3072]{1,0:T(8,128)(2,1)}, f32[1440,3072]{1,0:T(8,128)}, f32[1440,3072]{1,0:T(8,128)}) fusion(f32[3072]{0:T(1024)S(1)} %reshape.382, bf16[768,3072]{1,0:T(8,128)(2,1)S(1)} %bitcast.185, f32[1440,768]{1,0:T(8,128)S(1)} %get-tuple-element.108, f32[768]{0:T(1024)S(1)} %reshape.381, f32[768]{0:T(1024)S(1)} %reshape.380, ...), kind=kOutput, calls=%fused_computation.6 | convolution fusion | flops 7092264960 | bytes 53409024 | tf_op jit(solution)/shard_map/dot_general | solution.py:173
  376.3 21.3 %convert_reduce_fusion = (f32[3072]{0:T(1024)}, bf16[1440,3072]{1,0:T(8,128)(2,1)}) fusion(f32[1440,3072]{1,0:T(8,128)} %get-tuple-element.76, bf16[3072,768]{0,1:T(8,128)(2,1)S(1)} %bitcast.184, bf16[640,768]{1,0:T(8,128)(2,1)} %bitcast.187, bf16[800,768]{1,0:T(8,128)(2,1)S(1)} %bitcast.177, f32[1440,3072]{1,0:T(8,128)} %get-tuple-element.109, ...), kind=kOutput, calls=%fused_computation.4 | convolution fusion | flops 6874395648 | bytes 51191808 | tf_op jit(solution)/shard_map/tj,ij->ti/dot_general | solution.py:182
  397.6 13.7 %multiply_reduce_fusion.1 = (f32[768]{0:T(1024)}, f32[1440]{0:T(1024)S(1)}, f32[768]{0:T(1024)}, f32[1440,768]{1,0:T(8,128)S(1)}) fusion(f32[1440,768]{1,0:T(8,128)S(1)} %get-tuple-element.108, f32[1440]{0:T(1024)S(1)} %fusion.104, f32[1440]{0:T(1024)S(1)} %broadcast_multiply_fusion, f32[768]{0:T(1024)S(1)} %reshape.380, ...), kind=kOutput, calls=%fused_computation.67 | convolution fusion | flops 6803616768 | bytes 22439808 | tf_op jit(solution)/shard_map/tj,ij->ti/dot_general | solution.py:187
  434.6 10.0 %convert_bitcast_fusion.2 = bf16[16,40,1,12,64]{4,1,3,0,2:T(8,128)(2,1)} fusion(f32[16,12,40,40]{2,3,1,0:T(8,128)} %fusion.100, f32[16,12,40,40]{2,3,1,0:T(8,128)} %copy-done.8, f32[16,12,40]{2,1,0:T(8,128)S(1)} %copy-done.35, bf16[16,40,1,12,64]{4,3,2,1,0:T(8,128)(2,1)} %copy-done.26), kind=kOutput, calls=%fused_computation.98 | convolution fusion | flops 41971240 | bytes 4454400 | tf_op jit(solution)/shard_map/chqk,ckhd->cqhd/dot_general | solution.py:59
  444.6 9.2 %convert_bitcast_fusion.1 = bf16[16,40,1,12,64]{4,1,3,0,2:T(8,128)(2,1)} fusion(f32[16,12,40,40]{2,3,1,0:T(8,128)} %fusion.100, f32[16,12,40,40]{2,3,1,0:T(8,128)} %copy-done.8, f32[16,12,40]{2,1,0:T(8,128)S(1)} %copy-done.35, bf16[16,40,1,12,64]{4,3,2,1,0:T(8,128)(2,1)S(1)} %copy-done.25), kind=kOutput, calls=%fused_computation.97 | convolution fusion | flops 41971240 | bytes 4454400 | tf_op jit(solution)/shard_map/chqk,cqhd->ckhd/dot_general | solution.py:62
  475.5 19.7 %fusion.92 = bf16[4,200,1,12,64]{1,4,3,0,2:T(8,128)(2,1)} fusion(f32[4,12,200,200]{2,3,1,0:T(8,128)} %fusion.81, f32[4,12,200]{2,1,0:T(8,128)S(1)} %copy-done.46, f32[4,12,200,200]{2,3,1,0:T(8,128)} %copy-done.3, pred[4,200]{1,0:T(4,128)(4,1)S(1)} %copy-done.52, bf16[4,200,1,12,64]{1,4,3,0,2:T(8,128)(2,1)S(1)} %copy-done.17), kind=kOutput, calls=%fused_computation.122 | convolution fusion | flops 267504192 | bytes 17856800 | tf_op jit(solution)/shard_map/chqk,ckhd->cqhd/dot_general | solution.py:59
  495.2 19.0 %fusion.87 = bf16[4,200,1,12,64]{1,4,3,0,2:T(8,128)(2,1)} fusion(f32[4,12,200,200]{2,3,1,0:T(8,128)} %fusion.81, f32[4,12,200]{2,1,0:T(8,128)S(1)} %copy-done.46, f32[4,12,200,200]{2,3,1,0:T(8,128)} %copy-done.3, pred[4,200]{1,0:T(4,128)(4,1)S(1)} %copy-done.52, bf16[4,200,1,12,64]{1,4,3,0,2:T(8,128)(2,1)S(1)} %copy-done.15), kind=kOutput, calls=%fused_computation.121 | convolution fusion | flops 267504192 | bytes 17856800 | tf_op jit(solution)/shard_map/chqk,cqhd->ckhd/dot_general | solution.py:62
  528.6 12.8 %copy.203 = bf16[16,40,3,12,64]{1,0,4,3,2:T(8,128)(2,1)} copy(bf16[16,40,3,12,64]{4,1,3,0,2:T(8,128)(2,1)} %pad_maximum_fusion.2) | data formatting | bytes 5898240 | tf_op jit(solution)/shard_map/convert_element_type | solution.py:69
  541.3 14.1 %reshape.397 = bf16[640,2304]{0,1:T(8,128)(2,1)} reshape(bf16[16,40,3,12,64]{1,0,4,3,2:T(8,128)(2,1)} %copy.203) | data formatting | bytes 5898240 | tf_op jit(solution)/shard_map/convert_element_type | solution.py:69
  564.8 9.7 %convert_element_type.280 = bf16[800,2304]{0,1:T(8,128)(2,1)} reshape(bf16[4,200,3,12,64]{1,0,4,3,2:T(4,128)(2,1)} %copy.184) | data formatting | bytes 7372800 | tf_op jit(solution)/shard_map/convert_element_type | solution.py:69
  574.5 12.6 %convolution_convert_fusion = bf16[768,2304]{1,0:T(8,128)(2,1)} fusion(bf16[640,2304]{0,1:T(8,128)(2,1)} %reshape.397, bf16[800,2304]{0,1:T(8,128)(2,1)} %convert_element_type.280, f32[768]{0:T(1024)S(1)} %copy-done.54, f32[768]{0:T(1024)S(1)} %copy-done.48, f32[1440]{0:T(1024)S(1)} %copy-done.39, f32[1440]{0:T(1024)S(1)} %copy-done.37, ...), kind=kOutput, calls=%fused_computation.48 | convolution fusion | flops 5121073152 | bytes 12403968 | tf_op jit(solution)/shard_map/ti,tj->ij/dot_general | solution.py:203
  587.1 9.1 %reshape.369 = bf16[8,96,4,576]{3,2,1,0:T(4,128)(2,1)} reshape(bf16[768,2304]{1,0:T(8,128)(2,1)} %convolution_convert_fusion) | data formatting | bytes 7077888 | tf_op jit(solution)/shard_map/reshape | solution.py:95
  614.8 12.5 %convolution_convert_fusion.1 = bf16[3072,768]{1,0:T(8,128)(2,1)} fusion(bf16[1440,3072]{1,0:T(8,128)(2,1)} %get-tuple-element.75, bf16[640,768]{1,0:T(8,128)(2,1)} %bitcast.188, bf16[800,768]{1,0:T(8,128)(2,1)S(1)} %bitcast.179), kind=kOutput, calls=%fused_computation.49 | convolution fusion | flops 6801555456 | bytes 15777792 | tf_op jit(solution)/shard_map/ti,tj->ij/dot_general | solution.py:180
  639.7 14.1 %convolution_convert_fusion.2 = bf16[768,3072]{1,0:T(8,128)(2,1)} fusion(bf16[1440,3072]{1,0:T(8,128)(2,1)} %get-tuple-element.113, f32[1440,768]{1,0:T(8,128)} %copy-done.6, f32[768]{0:T(1024)S(1)} %copy-done.56, f32[768]{0:T(1024)S(1)} %reshape.380, f32[1440]{0:T(1024)S(1)} %fusion.104, f32[1440]{0:T(1024)S(1)} %broadcast_multiply_fusion), kind=kOutput, calls=%fused_computation.50 | convolution fusion | flops 6802661376 | bytes 18007296 | tf_op jit(solution)/shard_map/ti,tj->ij/dot_general | solution.py:185
  653.8 9.8 %reshape.373 = bf16[8,96,4,768]{3,2,1,0:T(4,128)(2,1)} reshape(bf16[768,3072]{1,0:T(8,128)(2,1)} %convolution_convert_fusion.2) | data formatting | bytes 9437184 | tf_op jit(solution)/shard_map/reshape | solution.py:95
  669.0 9.3 %reshape.374 = bf16[32,576,128]{2,1,0:T(8,128)(2,1)} reshape(bf16[8,4,96,768]{3,2,1,0:T(8,128)(2,1)} %bitcast.162) | data formatting | bytes 9437184 | tf_op jit(solution)/shard_map/reshape | solution.py:96
  678.3 9.3 %copy.194 = bf16[8,4,384,192]{3,2,1,0:T(8,128)(2,1)} copy(bf16[8,4,384,192]{2,0,3,1:T(8,128)(2,1)} %bitcast.163) | data formatting | bytes 9437184 | tf_op jit(solution)/shard_map/transpose | solution.py:95
  687.6 12.0 %reshape.376 = bf16[32,576,128]{2,1,0:T(8,128)(2,1)} reshape(bf16[8,4,384,192]{3,2,1,0:T(8,128)(2,1)} %copy.194) | data formatting | bytes 9437184 | tf_op jit(solution)/shard_map/reshape | solution.py:96
  708.4 13.1 %add_convert_fusion.2 = bf16[1440,768]{1,0:T(8,128)(2,1)S(1)} fusion(f32[1440,768]{1,0:T(8,128)} %copy-done.6, bf16[1440,3072]{1,0:T(8,128)(2,1)} %get-tuple-element.75, bf16[3072,768]{0,1:T(8,128)(2,1)} %bitcast.181, f32[768]{0:T(1024)S(1)} %reshape.383), kind=kOutput, calls=%fused_computation.71 | convolution fusion | flops 6798090240 | bytes 20204544 | tf_op jit(solution)/shard_map/dot_general | solution.py:176
  723.6 11.4 %fusion.131 = (f32[768]{0:T(1024)S(1)}, f32[1440]{0:T(1024)S(1)}, f32[1440,768]{1,0:T(8,128)S(1)}) fusion(f32[768]{0:T(1024)S(1)} %copy-done.48, f32[1440]{0:T(1024)S(1)} %copy-done.37, bf16[640,768]{1,0:T(8,128)(2,1)S(1)} %bitcast.172, bf16[800,768]{1,0:T(8,128)(2,1)S(1)} %bitcast.156, bf16[768,2304]{1,0:T(8,128)(2,1)} %reshape.351, ...), kind=kOutput, calls=%fused_computation.185 | convolution fusion | flops 5119301120 | bytes 16827648 | tf_op jit(solution)/shard_map/tj,ij->ti/dot_general | solution.py:210
  749.7 39.8 %psum.7 = f32[9216]{0:T(1024)S(1)} all-reduce(f32[9216]{0:T(1024)S(1)} %constant_dynamic-update-slice_fusion), channel_id=1, replica_groups=mesh['img'=8,'seq'=4] {'img','seq'}, use_global_device_ids=true, to_apply=%region_22.23 | all-reduce | flops 9216 | bytes 73728 | tf_op jit(solution)/shard_map/psum | solution.py:225
  794.7 66.3 %reduce-scatter.5.cloned.1.call-done = bf16[1,1152,128]{2,1,0:T(8,128)(2,1)} async-done(((bf16[32,1152,128]{2,1,0:T(8,128)(2,1)}), bf16[1,1152,128]{2,1,0:T(8,128)(2,1)}) %reduce-scatter.5.cloned.1.call-update) | async-done | bytes 294928 | tf_op jit(solution)/shard_map/reduce_scatter | solution.py:98
  (293 shorter events, 298.7 us)
Async XLA Ops:
  7.2 15.2 %copy-start = (s32[64,40]{0,1:T(8,128)S(1)}, s32[64,40]{0,1:T(8,128)}, u32[]{:S(2)}) copy-start(s32[64,40]{0,1:T(8,128)} %param.21) | copy-start | bytes 30724
  7.2 15.3 %copy-start.10 = (bf16[16,40,768]{2,1,0:T(8,128)(2,1)S(1)}, bf16[16,40,768]{2,1,0:T(8,128)(2,1)}, u32[]{:S(2)}) copy-start(bf16[16,40,768]{2,1,0:T(8,128)(2,1)} %param.19) | copy-start | bytes 2949124
  7.2 15.3 %copy-start.4 = (bf16[4,200,768]{2,1,0:T(8,128)(2,1)S(1)}, bf16[4,200,768]{2,1,0:T(8,128)(2,1)}, u32[]{:S(2)}) copy-start(bf16[4,200,768]{2,1,0:T(8,128)(2,1)} %param.18) | copy-start | bytes 3686404
  7.2 73.8 %all-gather.7.cloned.1.call-start = ((), (), s32[]{:S(2)}) async-start(), calls=%async_computation.4 | async-start | bytes 4325376 | tf_op jit(solution)/shard_map/all_gather | solution.py:76
  16.0 205.4 %all-gather.9.cloned.1.call-start = ((), (), s32[]{:S(2)}) async-start(), calls=%async_computation.5 | async-start | bytes 11354112 | tf_op jit(solution)/shard_map/all_gather | solution.py:76
  22.3 769.2 %reduce-scatter.3.cloned.1.call-start = ((), (), s32[]{:S(2)}) async-start(), calls=%async_computation.2 | async-start | bytes 4866048 | tf_op jit(solution)/shard_map/reduce_scatter | solution.py:98
  23.6 185.4 %copy-start.51 = (pred[4,200]{1,0:T(4,128)(4,1)}, pred[4,200]{1,0:T(4,128)(4,1)S(1)}, u32[]{:S(2)}) copy-start(pred[4,200]{1,0:T(4,128)(4,1)S(1)} %dynamic-slice_compare_fusion) | copy-start | bytes 2404
  23.6 98.3 %copy-start.36 = (f32[1440]{0:T(1024)}, f32[1440]{0:T(1024)S(1)}, u32[]{:S(2)}) copy-start(f32[1440]{0:T(1024)S(1)} %broadcast_multiply_fusion.1) | copy-start | bytes 17284
  25.0 96.9 %copy-start.38 = (f32[1440]{0:T(1024)}, f32[1440]{0:T(1024)S(1)}, u32[]{:S(2)}) copy-start(f32[1440]{0:T(1024)S(1)} %fusion.103) | copy-start | bytes 17284
  84.5 37.5 %copy-start.53 = (f32[768]{0:T(1024)}, f32[768]{0:T(1024)S(1)}, u32[]{:S(2)}) copy-start(f32[768]{0:T(1024)S(1)} %reshape.378) | copy-start | bytes 9220
  84.7 37.3 %copy-start.47 = (f32[768]{0:T(1024)}, f32[768]{0:T(1024)S(1)}, u32[]{:S(2)}) copy-start(f32[768]{0:T(1024)S(1)} %reshape.377) | copy-start | bytes 9220
  136.4 191.7 %copy-start.55 = (f32[768]{0:T(1024)}, f32[768]{0:T(1024)S(1)}, u32[]{:S(2)}) copy-start(f32[768]{0:T(1024)S(1)} %reshape.381) | copy-start | bytes 9220
  324.6 51.7 %slice-start.2 = ((s8[4718592]{0:T(1024)(128)(4,1)}), s8[524288]{0:T(1024)(128)(4,1)S(1)}, s32[]{:S(2)}) async-start(s8[4718592]{0:T(1024)(128)(4,1)} %bitcast.182), calls=%async_computation.8 | async-start | bytes 1048576
  327.4 83.9 %copy-start.6 = (f32[1440,768]{1,0:T(8,128)}, f32[1440,768]{1,0:T(8,128)S(1)}, u32[]{:S(2)}) copy-start(f32[1440,768]{1,0:T(8,128)S(1)} %get-tuple-element.108) | copy-start | bytes 13271044
  328.1 48.2 %copy-start.44 = (f32[1440]{0:T(1024)}, f32[1440]{0:T(1024)S(1)}, u32[]{:S(2)}) copy-start(f32[1440]{0:T(1024)S(1)} %multiply_reduce_fusion.3) | copy-start | bytes 17284
  328.1 48.2 %copy-start.19 = (bf16[4,200,768]{2,1,0:T(8,128)(2,1)S(1)}, bf16[4,200,768]{2,1,0:T(8,128)(2,1)}, u32[]{:S(2)}) copy-start(bf16[4,200,768]{2,1,0:T(8,128)(2,1)} %param.34) | copy-start | bytes 3686404
  328.1 48.2 %slice-start.3 = ((s8[4718592]{0:T(1024)(128)(4,1)}), s8[4194304]{0:T(1024)(128)(4,1)S(1)}, s32[]{:S(2)}) async-start(s8[4718592]{0:T(1024)(128)(4,1)} %bitcast.182), calls=%async_computation.9 | async-start | bytes 8388608
  397.6 13.7 %copy-start.45 = (f32[1440]{0:T(1024)S(1)}, f32[1440]{0:T(1024)}, u32[]{:S(2)}) copy-start(f32[1440]{0:T(1024)} %copy-done.44) | copy-start | bytes 17284
  434.6 10.1 %copy-start.25 = (bf16[16,40,1,12,64]{4,3,2,1,0:T(8,128)(2,1)S(1)}, bf16[16,40,1,12,64]{4,3,2,1,0:T(8,128)(2,1)}, u32[]{:S(2)}) copy-start(bf16[16,40,1,12,64]{4,3,2,1,0:T(8,128)(2,1)} %copy-done.24) | copy-start | bytes 2949124
  475.5 19.7 %copy-start.15 = (bf16[4,200,1,12,64]{1,4,3,0,2:T(8,128)(2,1)S(1)}, bf16[4,200,1,12,64]{1,4,3,0,2:T(8,128)(2,1)}, u32[]{:S(2)}) copy-start(bf16[4,200,1,12,64]{1,4,3,0,2:T(8,128)(2,1)} %copy.213) | copy-start | bytes 3686404
  495.2 19.0 %copy-start.32 = (bf16[768,768]{1,0:T(8,128)(2,1)S(1)}, bf16[768,768]{1,0:T(8,128)(2,1)}, u32[]{:S(2)}) copy-start(bf16[768,768]{1,0:T(8,128)(2,1)} %convolution_convert_fusion.4) | copy-start | bytes 3538948
  541.3 14.1 %copy-start.27 = (bf16[4,200,1,12,64]{1,4,3,0,2:T(8,128)(2,1)S(1)}, bf16[4,200,1,12,64]{1,4,3,0,2:T(8,128)(2,1)}, u32[]{:S(2)}) copy-start(bf16[4,200,1,12,64]{1,4,3,0,2:T(8,128)(2,1)} %fusion.97) | copy-start | bytes 3686404
  564.7 9.8 %copy-start.37 = (f32[1440]{0:T(1024)S(1)}, f32[1440]{0:T(1024)}, u32[]{:S(2)}) copy-start(f32[1440]{0:T(1024)} %copy-done.36) | copy-start | bytes 17284
  564.7 9.8 %copy-start.39 = (f32[1440]{0:T(1024)S(1)}, f32[1440]{0:T(1024)}, u32[]{:S(2)}) copy-start(f32[1440]{0:T(1024)} %copy-done.38) | copy-start | bytes 17284
  564.7 9.8 %copy-start.48 = (f32[768]{0:T(1024)S(1)}, f32[768]{0:T(1024)}, u32[]{:S(2)}) copy-start(f32[768]{0:T(1024)} %copy-done.47) | copy-start | bytes 9220
  564.8 9.8 %copy-start.54 = (f32[768]{0:T(1024)S(1)}, f32[768]{0:T(1024)}, u32[]{:S(2)}) copy-start(f32[768]{0:T(1024)} %copy-done.53) | copy-start | bytes 9220
  613.6 247.5 %reduce-scatter.5.cloned.1.call-start = ((), (), s32[]{:S(2)}) async-start(), calls=%async_computation.3 | async-start | bytes 9732096 | tf_op jit(solution)/shard_map/reduce_scatter | solution.py:98
  708.4 15.2 %copy-start.7 = (bf16[800,2304]{0,1:T(8,128)(2,1)S(1)}, bf16[800,2304]{0,1:T(8,128)(2,1)}, u32[]{:S(2)}) copy-start(bf16[800,2304]{0,1:T(8,128)(2,1)} %convert_element_type.280) | copy-start | bytes 11059204
  722.5 16.6 %slice-start = ((s8[4423680]{0:T(1024)(128)(4,1)}), s8[4194304]{0:T(1024)(128)(4,1)S(1)}, s32[]{:S(2)}) async-start(s8[4423680]{0:T(1024)(128)(4,1)} %bitcast.148), calls=%async_computation.6 | async-start | bytes 8388608
  723.6 11.4 %copy-start.43 = (f32[1440]{0:T(1024)S(1)}, f32[1440]{0:T(1024)}, u32[]{:S(2)}) copy-start(f32[1440]{0:T(1024)} %copy-done.42) | copy-start | bytes 17284
  723.6 15.5 %slice-start.1 = ((s8[4423680]{0:T(1024)(128)(4,1)}), s8[229376]{0:T(1024)(128)(4,1)S(1)}, s32[]{:S(2)}) async-start(s8[4423680]{0:T(1024)(128)(4,1)} %bitcast.148), calls=%async_computation.7 | async-start | bytes 458752
  745.3 118.5 %copy-start.1 = (s32[64,40]{0,1:T(8,128)S(1)}, s32[64,40]{0,1:T(8,128)}, u32[]{:S(2)}) copy-start(s32[64,40]{0,1:T(8,128)} %param.21) | copy-start | bytes 30724
  (35 other events, 149.7 us)
Sparse Core Ops, SparseCore 0:
  16.2 64.7 all-gather.6
  84.4 87.4 all-gather.8
  613.7 105.7 reduce-scatter.2
  726.2 134.7 reduce-scatter.4
where the time goes:
time: 880 us; the launch traced here: 871 us
  local copies, waits for them, and re-layouts  376 us (43%)
  matrix products  256 us (29%)
  waiting for transfers between devices  122 us (14%)
  other arithmetic  62.1 us (7%)
  blocking collectives  39.8 us (5%)
  between operations  14.9 us (2%)
    reduce_scatter x2, waiting for transfers between devices, scatter_mats(): mine = lax.psum_scatter(flat, AXES, scatter_dimension=0, tiled=False)  66.3 us
    all_gather x2, waiting for transfers between devices, gather_mats(): whole = lax.all_gather(flat, AXES, axis=0, tiled=False)  55.9 us
    slice x7, local copies, waits for them, and re-layouts, gather_mats(): piece = whole[:, at:at + rows].reshape((n_img, n_seq) + m.shape)  52.6 us
    dot_general x1, matrix products, body(): jnp.dot(input_two, up_full, preferred_element_type=jnp.float32) + bias_up  48.1 us
    reshape x4, local copies, waits for them, and re-layouts, gather_mats(): piece = whole[:, at:at + rows].reshape((n_img, n_seq) + m.shape)  44.4 us
    psum x1, blocking collectives, body(): vector_sums = lax.psum(jnp.concatenate(vectors), AXES)  39.8 us
    unnamed x144, local copies, waits for them, and re-layouts  36.7 us
    convert_element_type x3, local copies, waits for them, and re-layouts, attend_back(): jnp.stack([grad_query, grad_key, grad_value], axis=2).astype(jnp.bfloat16)  36.6 us
  transfers between devices with their start and end apart: 4, of which 2 were waited for; matrix products, arithmetic and copies ran while one was open for 33% of the time, Pallas kernels for 0%

commit v1 on v0

--- a/solution.py
+++ b/solution.py
@@ -222,7 +222,9 @@
         grad_bias_up,
         grad_bias_down,
     )
-    vector_sums = lax.psum(jnp.concatenate(vectors), AXES)
+    block = jnp.concatenate(vectors)
+    terms = lax.all_gather(block, AXES, axis=0, tiled=False)
+    vector_sums = terms.sum(axis=0)
     vec_out, at = ([], 0)
     for v in vectors:
         width = v.shape[0] // n_seq

time: 880 us -> 917 us (1.042)
  waiting for transfers between devices: 122 us -> 186 us
  blocking collectives: 39.8 us -> 0 us
    reduce_scatter x2, waiting for transfers between devices: 66.3 us -> 130 us  [scatter_mats(): mine = lax.psum_scatter(flat, AXES, scatter_dimension=0, tiled=False)]
    psum x1 -> x0, blocking collectives: 39.8 us -> none  [body(): vector_sums = lax.psum(jnp.concatenate(vectors), AXES)]
    unnamed x144 -> x142, local copies, waits for them, and re-layouts: 36.7 us -> 36.8 us
  transfers between devices with their start and end apart: 4 -> 5, of which waited for: 2 -> 2; matrix products, arithmetic and copies ran while one was open for 33% -> 35% of each run, Pallas kernels for 0% -> 0%
where the time goes in v1:
time: 917 us; the launch traced here: 907 us
  local copies, waits for them, and re-layouts  379 us (41%)
  matrix products  261 us (28%)
  waiting for transfers between devices  186 us (20%)
  other arithmetic  65.1 us (7%)
  between operations  15 us (2%)
    reduce_scatter x2, waiting for transfers between devices, scatter_mats(): mine = lax.psum_scatter(flat, AXES, scatter_dimension=0, tiled=False)  130 us
    all_gather x2, waiting for transfers between devices, gather_mats(): whole = lax.all_gather(flat, AXES, axis=0, tiled=False)  55.9 us
    slice x7, local copies, waits for them, and re-layouts, gather_mats(): piece = whole[:, at:at + rows].reshape((n_img, n_seq) + m.shape)  52.4 us
    dot_general x1, matrix products, body(): jnp.dot(input_two, up_full, preferred_element_type=jnp.float32) + bias_up  48.3 us
    reshape x4, local copies, waits for them, and re-layouts, gather_mats(): piece = whole[:, at:at + rows].reshape((n_img, n_seq) + m.shape)  44.5 us
    unnamed x142, local copies, waits for them, and re-layouts  36.8 us
    reshape x6, local copies, waits for them, and re-layouts, scatter_mats(): m.astype(jnp.bfloat16).reshape(n_img, rows, n_seq, cols)  36.5 us
    convert_element_type x3, local copies, waits for them, and re-layouts, attend_back(): jnp.stack([grad_query, grad_key, grad_value], axis=2).astype(jnp.bfloat16)  36.4 us
  transfers between devices with their start and end apart: 5, of which 2 were waited for; matrix products, arithmetic and copies ran while one was open for 35% of the time, Pallas kernels for 0%

profile of v1, /device:TPU:0, one launch (start us, length us, event | category | flops | bytes accessed | tf_op | source)
XLA Modules:
  0.0 906.9 jit_solution(3664651061660328891)
XLA Ops:
  25.1 55.9 %all-gather.11.cloned.1.call-done = bf16[32,900,64]{1,2,0:T(8,128)(2,1)} async-done(((bf16[1,900,64]{1,2,0:T(8,128)(2,1)}), bf16[32,900,64]{1,2,0:T(8,128)(2,1)}) %all-gather.11.cloned.1.call-update) | async-done | bytes 3686416 | tf_op jit(solution)/shard_map/all_gather | solution.py:76
  96.9 10.8 %reshape.350 = bf16[8,4,96,576]{3,2,1,0:T(8,128)(2,1)} reshape(bf16[32,864,64]{2,1,0:T(8,128)(2,1)} %copy.194) | data formatting | bytes 7077888 | tf_op jit(solution)/shard_map/reshape | solution.py:80
  121.7 9.1 %fusion.8 = bf16[1440,2304]{1,0:T(8,128)(2,1)S(1)} fusion(bf16[768,2304]{1,0:T(8,128)(2,1)} %reshape.351, f32[2304]{0:T(1024)S(1)} %pad_maximum_fusion.12, f32[768]{0:T(1024)S(1)} %reshape.378, f32[768]{0:T(1024)S(1)} %reshape.377, f32[1440]{0:T(1024)S(1)} %fusion.103, f32[1440]{0:T(1024)S(1)} %broadcast_multiply_fusion.1, ...), kind=kOutput, calls=%fused_computation.22 | convolution fusion | flops 5112668160 | bytes 12413184 | tf_op jit(solution)/shard_map/dot_general | solution.py:163
  136.4 9.8 %reshape_reshape.9 = bf16[16,40,3,12,64]{4,3,2,1,0:T(8,128)(2,1)} reshape(bf16[640,2304]{1,0:T(8,128)(2,1)} %slice.190) | data formatting | bytes 5898240 | tf_op jit(solution)/shard_map/reshape;reshape | solution.py:26
  168.2 12.1 %reshape.399 = bf16[4,200,3,12,64]{4,3,2,1,0:T(8,128)(2,1)} reshape(bf16[800,2304]{1,0:T(8,128)(2,1)} %slice.186) | data formatting | bytes 7372800 | tf_op jit(solution)/shard_map/reshape;reshape | solution.py:26
  239.4 14.1 %fusion.135 = (bf16[32,1152,64]{1,2,0:T(8,128)(2,1)}, bf16[32,1152,64]{1,2,0:T(8,128)(2,1)}) fusion(bf16[32,2592,64]{1,2,0:T(8,128)(2,1)} %all-gather.13.cloned.1.call-done), kind=kLoop, calls=%fused_computation.187 | loop fusion | bytes 18874368 | tf_op jit(solution)/shard_map/slice | solution.py:80
  253.5 9.7 %copy.225 = bf16[32,1152,64]{2,1,0:T(8,128)(2,1)} copy(bf16[32,1152,64]{1,2,0:T(8,128)(2,1)} %get-tuple-element.93) | data formatting | bytes 9437184 | tf_op jit(solution)/shard_map/slice | solution.py:80
  263.2 15.5 %reshape.361 = bf16[8,4,384,192]{3,2,1,0:T(8,128)(2,1)} reshape(bf16[32,1152,64]{2,1,0:T(8,128)(2,1)} %copy.225) | data formatting | bytes 9437184 | tf_op jit(solution)/shard_map/reshape | solution.py:80
  278.7 8.8 copy.226
  293.1 9.7 %copy.221 = bf16[32,1152,64]{2,1,0:T(8,128)(2,1)} copy(bf16[32,1152,64]{1,2,0:T(8,128)(2,1)} %get-tuple-element.94) | data formatting | bytes 9437184 | tf_op jit(solution)/shard_map/slice | solution.py:80
  302.8 13.4 %reshape.359 = bf16[8,4,96,768]{3,2,1,0:T(8,128)(2,1)} reshape(bf16[32,1152,64]{2,1,0:T(8,128)(2,1)} %copy.221) | data formatting | bytes 9437184 | tf_op jit(solution)/shard_map/reshape | solution.py:80
  327.7 48.3 %multiply_convert_fusion = (bf16[1440,3072]{1,0:T(8,128)(2,1)}, f32[1440,3072]{1,0:T(8,128)}, f32[1440,3072]{1,0:T(8,128)}) fusion(f32[3072]{0:T(1024)S(1)} %reshape.382, bf16[768,3072]{1,0:T(8,128)(2,1)S(1)} %bitcast.187, f32[1440,768]{1,0:T(8,128)S(1)} %get-tuple-element.124, f32[768]{0:T(1024)S(1)} %reshape.381, f32[768]{0:T(1024)S(1)} %reshape.380, ...), kind=kOutput, calls=%fused_computation.6 | convolution fusion | flops 7092264960 | bytes 53409024 | tf_op jit(solution)/shard_map/dot_general | solution.py:173
  376.1 20.8 %convert_reduce_fusion = (f32[3072]{0:T(1024)S(1)}, bf16[1440,3072]{1,0:T(8,128)(2,1)}) fusion(f32[1440,3072]{1,0:T(8,128)} %get-tuple-element.92, bf16[3072,768]{0,1:T(8,128)(2,1)S(1)} %bitcast.186, bf16[640,768]{1,0:T(8,128)(2,1)} %bitcast.189, bf16[800,768]{1,0:T(8,128)(2,1)S(1)} %bitcast.179, f32[1440,3072]{1,0:T(8,128)} %get-tuple-element.125, ...), kind=kOutput, calls=%fused_computation.4 | convolution fusion | flops 6874395648 | bytes 51191808 | tf_op jit(solution)/shard_map/tj,ij->ti/dot_general | solution.py:182
  396.8 13.5 %multiply_reduce_fusion.1 = (f32[768]{0:T(1024)}, f32[1440]{0:T(1024)S(1)}, f32[768]{0:T(1024)S(1)}, f32[1440,768]{1,0:T(8,128)S(1)}) fusion(f32[1440,768]{1,0:T(8,128)S(1)} %get-tuple-element.124, f32[1440]{0:T(1024)S(1)} %fusion.104, f32[1440]{0:T(1024)S(1)} %broadcast_multiply_fusion, f32[768]{0:T(1024)S(1)} %reshape.380, ...), kind=kOutput, calls=%fused_computation.67 | convolution fusion | flops 6803616768 | bytes 22439808 | tf_op jit(solution)/shard_map/tj,ij->ti/dot_general | solution.py:187
  429.5 10.1 %convert_bitcast_fusion.2 = bf16[16,40,1,12,64]{4,1,3,0,2:T(8,128)(2,1)} fusion(f32[16,12,40,40]{2,3,1,0:T(8,128)} %fusion.100, f32[16,12,40,40]{2,3,1,0:T(8,128)} %copy-done.7, f32[16,12,40]{2,1,0:T(8,128)S(1)} %copy-done.34, bf16[16,40,1,12,64]{4,3,2,1,0:T(8,128)(2,1)} %copy-done.26), kind=kOutput, calls=%fused_computation.98 | convolution fusion | flops 41971240 | bytes 4454400 | tf_op jit(solution)/shard_map/chqk,ckhd->cqhd/dot_general | solution.py:59
  439.6 9.1 %convert_bitcast_fusion.1 = bf16[16,40,1,12,64]{4,1,3,0,2:T(8,128)(2,1)} fusion(f32[16,12,40,40]{2,3,1,0:T(8,128)} %fusion.100, f32[16,12,40,40]{2,3,1,0:T(8,128)} %copy-done.7, f32[16,12,40]{2,1,0:T(8,128)S(1)} %copy-done.34, bf16[16,40,1,12,64]{4,3,2,1,0:T(8,128)(2,1)S(1)} %copy-done.25), kind=kOutput, calls=%fused_computation.97 | convolution fusion | flops 41971240 | bytes 4454400 | tf_op jit(solution)/shard_map/chqk,cqhd->ckhd/dot_general | solution.py:62
  470.4 19.7 %fusion.92 = bf16[4,200,1,12,64]{1,4,3,0,2:T(8,128)(2,1)} fusion(f32[4,12,200,200]{2,3,1,0:T(8,128)} %fusion.81, f32[4,12,200]{2,1,0:T(8,128)S(1)} %copy-done.44, f32[4,12,200,200]{2,3,1,0:T(8,128)} %copy-done.3, pred[4,200]{1,0:T(4,128)(4,1)S(1)} %copy-done.50, bf16[4,200,1,12,64]{1,4,3,0,2:T(8,128)(2,1)S(1)} %copy-done.15), kind=kOutput, calls=%fused_computation.122 | convolution fusion | flops 267504192 | bytes 17856800 | tf_op jit(solution)/shard_map/chqk,ckhd->cqhd/dot_general | solution.py:59
  490.1 19.4 %fusion.87 = bf16[4,200,1,12,64]{1,4,3,0,2:T(8,128)(2,1)} fusion(f32[4,12,200,200]{2,3,1,0:T(8,128)} %fusion.81, f32[4,12,200]{2,1,0:T(8,128)S(1)} %copy-done.44, f32[4,12,200,200]{2,3,1,0:T(8,128)} %copy-done.3, pred[4,200]{1,0:T(4,128)(4,1)S(1)} %copy-done.50, bf16[4,200,1,12,64]{1,4,3,0,2:T(8,128)(2,1)} %copy.264), kind=kOutput, calls=%fused_computation.121 | convolution fusion | flops 267504192 | bytes 17856800 | tf_op jit(solution)/shard_map/chqk,cqhd->ckhd/dot_general | solution.py:62
  515.4 12.7 %copy.254 = bf16[16,40,3,12,64]{1,0,4,3,2:T(8,128)(2,1)} copy(bf16[16,40,3,12,64]{4,1,3,0,2:T(8,128)(2,1)} %pad_maximum_fusion.2) | data formatting | bytes 5898240 | tf_op jit(solution)/shard_map/convert_element_type | solution.py:69
  528.1 14.1 %reshape.398 = bf16[640,2304]{0,1:T(8,128)(2,1)} reshape(bf16[16,40,3,12,64]{1,0,4,3,2:T(8,128)(2,1)} %copy.254) | data formatting | bytes 5898240 | tf_op jit(solution)/shard_map/convert_element_type | solution.py:69
  551.3 9.6 %convert_element_type.280 = bf16[800,2304]{0,1:T(8,128)(2,1)} reshape(bf16[4,200,3,12,64]{1,0,4,3,2:T(4,128)(2,1)} %copy.235) | data formatting | bytes 7372800 | tf_op jit(solution)/shard_map/convert_element_type | solution.py:69
  567.7 14.5 %fusion.131 = (f32[768]{0:T(1024)S(1)}, f32[1440]{0:T(1024)S(1)}, f32[1440,768]{1,0:T(8,128)S(1)}) fusion(f32[768]{0:T(1024)S(1)} %copy-done.48, f32[1440]{0:T(1024)S(1)} %copy-done.37, bf16[640,768]{1,0:T(8,128)(2,1)S(1)} %bitcast.173, bf16[800,768]{1,0:T(8,128)(2,1)S(1)} %bitcast.155, bf16[768,2304]{1,0:T(8,128)(2,1)} %reshape.351, ...), kind=kOutput, calls=%fused_computation.185 | convolution fusion | flops 5119301120 | bytes 16827648 | tf_op jit(solution)/shard_map/tj,ij->ti/dot_general | solution.py:210
  608.9 12.4 %convolution_convert_fusion = bf16[768,2304]{1,0:T(8,128)(2,1)} fusion(bf16[640,2304]{0,1:T(8,128)(2,1)} %reshape.398, bf16[800,2304]{0,1:T(8,128)(2,1)} %convert_element_type.280, f32[768]{0:T(1024)S(1)} %copy-done.52, f32[768]{0:T(1024)S(1)} %copy-done.48, f32[1440]{0:T(1024)S(1)} %copy-done.39, f32[1440]{0:T(1024)S(1)} %copy-done.37, ...), kind=kOutput, calls=%fused_computation.48 | convolution fusion | flops 5121073152 | bytes 12403968 | tf_op jit(solution)/shard_map/ti,tj->ij/dot_general | solution.py:203
  621.3 9.1 %reshape.369 = bf16[8,96,4,576]{3,2,1,0:T(4,128)(2,1)} reshape(bf16[768,2304]{1,0:T(8,128)(2,1)} %convolution_convert_fusion) | data formatting | bytes 7077888 | tf_op jit(solution)/shard_map/reshape | solution.py:95
  649.1 13.2 %convolution_convert_fusion.1 = bf16[3072,768]{1,0:T(8,128)(2,1)} fusion(bf16[1440,3072]{1,0:T(8,128)(2,1)} %get-tuple-element.91, bf16[640,768]{1,0:T(8,128)(2,1)S(1)} %bitcast.192, bf16[800,768]{1,0:T(8,128)(2,1)S(1)} %bitcast.182), kind=kOutput, calls=%fused_computation.49 | convolution fusion | flops 6801555456 | bytes 15777792 | tf_op jit(solution)/shard_map/ti,tj->ij/dot_general | solution.py:180
  675.0 13.5 %convolution_convert_fusion.2 = bf16[768,3072]{1,0:T(8,128)(2,1)} fusion(bf16[1440,3072]{1,0:T(8,128)(2,1)} %get-tuple-element.129, f32[1440,768]{1,0:T(8,128)S(1)} %bitcast.166, f32[768]{0:T(1024)S(1)} %copy-done.54, f32[768]{0:T(1024)S(1)} %reshape.380, f32[1440]{0:T(1024)S(1)} %fusion.104, f32[1440]{0:T(1024)S(1)} %broadcast_multiply_fusion), kind=kOutput, calls=%fused_computation.50 | convolution fusion | flops 6802661376 | bytes 18007296 | tf_op jit(solution)/shard_map/ti,tj->ij/dot_general | solution.py:185
  688.5 9.8 %reshape.373 = bf16[8,96,4,768]{3,2,1,0:T(4,128)(2,1)} reshape(bf16[768,3072]{1,0:T(8,128)(2,1)} %convolution_convert_fusion.2) | data formatting | bytes 9437184 | tf_op jit(solution)/shard_map/reshape | solution.py:95
  703.6 9.3 %reshape.374 = bf16[32,576,128]{2,1,0:T(8,128)(2,1)} reshape(bf16[8,4,96,768]{3,2,1,0:T(8,128)(2,1)} %bitcast.162) | data formatting | bytes 9437184 | tf_op jit(solution)/shard_map/reshape | solution.py:96
  712.9 9.1 %copy.245 = bf16[8,4,384,192]{3,2,1,0:T(8,128)(2,1)} copy(bf16[8,4,384,192]{2,0,3,1:T(8,128)(2,1)} %bitcast.163) | data formatting | bytes 9437184 | tf_op jit(solution)/shard_map/transpose | solution.py:95
  722.1 12.2 %reshape.376 = bf16[32,576,128]{2,1,0:T(8,128)(2,1)} reshape(bf16[8,4,384,192]{3,2,1,0:T(8,128)(2,1)} %copy.245) | data formatting | bytes 9437184 | tf_op jit(solution)/shard_map/reshape | solution.py:96
  743.0 13.1 %add_convert_fusion.2 = bf16[1440,768]{1,0:T(8,128)(2,1)S(1)} fusion(f32[1440,768]{1,0:T(8,128)} %copy-done.6, bf16[1440,3072]{1,0:T(8,128)(2,1)} %get-tuple-element.91, bf16[3072,768]{0,1:T(8,128)(2,1)} %bitcast.183, f32[768]{0:T(1024)S(1)} %reshape.383), kind=kOutput, calls=%fused_computation.71 | convolution fusion | flops 6798090240 | bytes 20204544 | tf_op jit(solution)/shard_map/dot_general | solution.py:176
  767.1 130.3 %reduce-scatter.5.cloned.1.call-done = bf16[1,1152,128]{2,1,0:T(8,128)(2,1)} async-done(((bf16[32,1152,128]{2,1,0:T(8,128)(2,1)}), bf16[1,1152,128]{2,1,0:T(8,128)(2,1)}) %reduce-scatter.5.cloned.1.call-update) | async-done | bytes 294928 | tf_op jit(solution)/shard_map/reduce_scatter | solution.py:98
  (296 shorter events, 299.4 us)
Async XLA Ops:
  7.2 15.2 %copy-start = (s32[64,40]{0,1:T(8,128)S(1)}, s32[64,40]{0,1:T(8,128)}, u32[]{:S(2)}) copy-start(s32[64,40]{0,1:T(8,128)} %param.21) | copy-start | bytes 30724
  7.2 15.3 %copy-start.9 = (bf16[16,40,768]{2,1,0:T(8,128)(2,1)S(1)}, bf16[16,40,768]{2,1,0:T(8,128)(2,1)}, u32[]{:S(2)}) copy-start(bf16[16,40,768]{2,1,0:T(8,128)(2,1)} %param.19) | copy-start | bytes 2949124
  7.2 15.3 %copy-start.4 = (bf16[4,200,768]{2,1,0:T(8,128)(2,1)S(1)}, bf16[4,200,768]{2,1,0:T(8,128)(2,1)}, u32[]{:S(2)}) copy-start(bf16[4,200,768]{2,1,0:T(8,128)(2,1)} %param.18) | copy-start | bytes 3686404
  7.2 73.8 %all-gather.11.cloned.1.call-start = ((), (), s32[]{:S(2)}) async-start(), calls=%async_computation.5 | async-start | bytes 4325376 | tf_op jit(solution)/shard_map/all_gather | solution.py:76
  16.0 205.1 %all-gather.13.cloned.1.call-start = ((), (), s32[]{:S(2)}) async-start(), calls=%async_computation.6 | async-start | bytes 11354112 | tf_op jit(solution)/shard_map/all_gather | solution.py:76
  22.3 738.0 %all-gather.9.cloned.1.call-start = ((), (), s32[]{:S(2)}) async-start(), calls=%async_computation.4 | async-start | bytes 1216512 | tf_op jit(solution)/shard_map/all_gather | solution.py:226
  23.6 185.1 %copy-start.49 = (pred[4,200]{1,0:T(4,128)(4,1)}, pred[4,200]{1,0:T(4,128)(4,1)S(1)}, u32[]{:S(2)}) copy-start(pred[4,200]{1,0:T(4,128)(4,1)S(1)} %dynamic-slice_compare_fusion) | copy-start | bytes 2404
  23.6 98.0 %copy-start.36 = (f32[1440]{0:T(1024)}, f32[1440]{0:T(1024)S(1)}, u32[]{:S(2)}) copy-start(f32[1440]{0:T(1024)S(1)} %broadcast_multiply_fusion.1) | copy-start | bytes 17284
  25.1 96.6 %copy-start.38 = (f32[1440]{0:T(1024)}, f32[1440]{0:T(1024)S(1)}, u32[]{:S(2)}) copy-start(f32[1440]{0:T(1024)S(1)} %fusion.103) | copy-start | bytes 17284
  84.5 37.2 %copy-start.51 = (f32[768]{0:T(1024)}, f32[768]{0:T(1024)S(1)}, u32[]{:S(2)}) copy-start(f32[768]{0:T(1024)S(1)} %reshape.378) | copy-start | bytes 9220
  84.7 37.0 %copy-start.47 = (f32[768]{0:T(1024)}, f32[768]{0:T(1024)S(1)}, u32[]{:S(2)}) copy-start(f32[768]{0:T(1024)S(1)} %reshape.377) | copy-start | bytes 9220
  136.0 191.6 %copy-start.53 = (f32[768]{0:T(1024)}, f32[768]{0:T(1024)S(1)}, u32[]{:S(2)}) copy-start(f32[768]{0:T(1024)S(1)} %reshape.381) | copy-start | bytes 9220
  324.2 51.9 %slice-start.4 = ((s8[4718592]{0:T(1024)(128)(4,1)}), s8[524288]{0:T(1024)(128)(4,1)S(1)}, s32[]{:S(2)}) async-start(s8[4718592]{0:T(1024)(128)(4,1)} %bitcast.184), calls=%async_computation.11 | async-start | bytes 1048576
  327.0 83.3 %copy-start.6 = (f32[1440,768]{1,0:T(8,128)}, f32[1440,768]{1,0:T(8,128)S(1)}, u32[]{:S(2)}) copy-start(f32[1440,768]{1,0:T(8,128)S(1)} %get-tuple-element.124) | copy-start | bytes 13271044
  327.7 48.4 %copy-start.42 = (f32[1440]{0:T(1024)}, f32[1440]{0:T(1024)S(1)}, u32[]{:S(2)}) copy-start(f32[1440]{0:T(1024)S(1)} %multiply_reduce_fusion.3) | copy-start | bytes 17284
  327.7 48.3 %copy-start.17 = (bf16[4,200,768]{2,1,0:T(8,128)(2,1)S(1)}, bf16[4,200,768]{2,1,0:T(8,128)(2,1)}, u32[]{:S(2)}) copy-start(bf16[4,200,768]{2,1,0:T(8,128)(2,1)} %param.34) | copy-start | bytes 3686404
  327.7 48.3 %slice-start.5 = ((s8[4718592]{0:T(1024)(128)(4,1)}), s8[4194304]{0:T(1024)(128)(4,1)S(1)}, s32[]{:S(2)}) async-start(s8[4718592]{0:T(1024)(128)(4,1)} %bitcast.184), calls=%async_computation.12 | async-start | bytes 8388608
  396.8 13.5 %copy-start.43 = (f32[1440]{0:T(1024)S(1)}, f32[1440]{0:T(1024)}, u32[]{:S(2)}) copy-start(f32[1440]{0:T(1024)} %copy-done.42) | copy-start | bytes 17284
  429.5 10.1 %copy-start.25 = (bf16[16,40,1,12,64]{4,3,2,1,0:T(8,128)(2,1)S(1)}, bf16[16,40,1,12,64]{4,3,2,1,0:T(8,128)(2,1)}, u32[]{:S(2)}) copy-start(bf16[16,40,1,12,64]{4,3,2,1,0:T(8,128)(2,1)} %copy-done.24) | copy-start | bytes 2949124
  490.1 19.4 %copy-start.13 = (bf16[16,40,1,12,64]{4,1,3,0,2:T(8,128)(2,1)S(1)}, bf16[16,40,1,12,64]{4,1,3,0,2:T(8,128)(2,1)}, u32[]{:S(2)}) copy-start(bf16[16,40,1,12,64]{4,1,3,0,2:T(8,128)(2,1)} %convert_bitcast_fusion) | copy-start | bytes 2949124
  528.1 14.2 %copy-start.28 = (bf16[4,200,1,12,64]{1,4,3,0,2:T(8,128)(2,1)S(1)}, bf16[4,200,1,12,64]{1,4,3,0,2:T(8,128)(2,1)}, u32[]{:S(2)}) copy-start(bf16[4,200,1,12,64]{1,4,3,0,2:T(8,128)(2,1)} %fusion.97) | copy-start | bytes 3686404
  528.1 14.2 %copy-start.29 = (bf16[4,200,1,12,64]{1,4,3,0,2:T(8,128)(2,1)S(1)}, bf16[4,200,1,12,64]{1,4,3,0,2:T(8,128)(2,1)}, u32[]{:S(2)}) copy-start(bf16[4,200,1,12,64]{1,4,3,0,2:T(8,128)(2,1)} %fusion.92) | copy-start | bytes 3686404
  560.9 25.5 %slice-start = ((s8[4423680]{0:T(1024)(128)(4,1)}), s8[4194304]{0:T(1024)(128)(4,1)S(1)}, s32[]{:S(2)}) async-start(s8[4423680]{0:T(1024)(128)(4,1)} %bitcast.148), calls=%async_computation.7 | async-start | bytes 8388608
  567.6 14.6 %copy-start.41 = (f32[1440]{0:T(1024)S(1)}, f32[1440]{0:T(1024)}, u32[]{:S(2)}) copy-start(f32[1440]{0:T(1024)} %copy-done.40) | copy-start | bytes 17284
  567.6 14.6 %copy-start.39 = (f32[1440]{0:T(1024)S(1)}, f32[1440]{0:T(1024)}, u32[]{:S(2)}) copy-start(f32[1440]{0:T(1024)} %copy-done.38) | copy-start | bytes 17284
  567.7 18.7 %slice-start.1 = ((s8[4423680]{0:T(1024)(128)(4,1)}), s8[229376]{0:T(1024)(128)(4,1)S(1)}, s32[]{:S(2)}) async-start(s8[4423680]{0:T(1024)(128)(4,1)} %bitcast.148), calls=%async_computation.8 | async-start | bytes 458752
  591.7 172.2 %reduce-scatter.3.cloned.1.call-start = ((), (), s32[]{:S(2)}) async-start(), calls=%async_computation.2 | async-start | bytes 4866048 | tf_op jit(solution)/shard_map/reduce_scatter | solution.py:98
  597.1 11.8 %copy-start.52 = (f32[768]{0:T(1024)S(1)}, f32[768]{0:T(1024)}, u32[]{:S(2)}) copy-start(f32[768]{0:T(1024)} %copy-done.51) | copy-start | bytes 9220
  635.0 8.0 copy-start.19
  647.9 249.4 %reduce-scatter.5.cloned.1.call-start = ((), (), s32[]{:S(2)}) async-start(), calls=%async_computation.3 | async-start | bytes 9732096 | tf_op jit(solution)/shard_map/reduce_scatter | solution.py:98
  662.3 12.7 %slice-start.2 = ((s8[4423680]{0:T(1024)(128)(4,1)}), s8[229376]{0:T(1024)(128)(4,1)S(1)}, s32[]{:S(2)}) async-start(s8[4423680]{0:T(1024)(128)(4,1)} %bitcast.165), calls=%async_computation.9 | async-start | bytes 458752
  758.2 141.9 %copy-start.1 = (s32[64,40]{0,1:T(8,128)S(1)}, s32[64,40]{0,1:T(8,128)}, u32[]{:S(2)}) copy-start(s32[64,40]{0,1:T(8,128)} %param.21) | copy-start | bytes 30724
  (35 other events, 135.2 us)
Sparse Core Ops, SparseCore 0:
  16.2 64.7 all-gather.10
  84.4 87.4 all-gather.12
  591.8 52.6 all-gather.8
  649.9 105.8 reduce-scatter.2
  762.5 134.7 reduce-scatter.4
